TPU v7x, 32 devices: a whole 2x2x4 slice. The times are simulated.
32 devices in a mesh: groups: 2 (over y), row: 8 (over z, x), col: 2 (over core).
Axes of the slice: x: 2, y: 2, z: 4, core: 2. Of those that a mesh axis runs over, the one named last changes fastest.
Arguments:
- object_slices: float32 [4, 2, 2048, 512], P(None, None, ('groups', 'row'), 'col'), parts along dimension 2, may hold values from -4 to 4
- probe: float32 [16, 2, 128, 128], P('groups'), parts along dimension 0, may hold values from -3 to 3
- taps: float32 [2, 63], replicated, may hold values from -0.5 to 0.5
- measured: float32 [64, 128, 128], P(('groups', 'row', 'col')), parts along dimension 0, may hold values from 0.5 to 16
- positions: int32 [64, 2], P(('groups', 'row', 'col')), parts along dimension 0, may hold values from -64 to 959, as said below
Outputs:
- object_grad: float32 [4, 2, 2048, 512], P(None, None, ('groups', 'row'), 'col'), parts along dimension 2
- new_probe: float32 [16, 2, 16384], P('groups', None, ('row', 'col')), parts along dimension 0
There are 2 independent parts, one for each index of `groups`. A program takes and returns all parts, laid end to end along the dimension named above; an argument that names none is the same for every part. Nothing has to cross between parts.
Inputs may be any that keep to these rules, and one draw needn't show every extreme that they name: `positions`: record r belongs to device d = r // 2 in row-major order over the (row, col) device grid, with tile indices (i, q); its row lies in [i * 128 - 128/2, (i + 1) * 128 - 128/2) and its column in [q * 256 - 128/2, (q + 1) * 256 - 128/2).
All inputs are finite; a program needn't handle non-finite values.
Results may differ from a plain program's by a relative error of at most 0.0003.
Values sent between devices are 32-bit elements; how exact they have to be, the bound alone decides.
No kernel may reach another device: no remote copies, remote signals or barrier semaphores. Data moves between devices by JAX's collectives and lax.ppermute only.
A program may use at most 64 MiB of HBM per device.

v0:
```python
import math
import jax
import jax.numpy as jnp
from jax import lax
from jax.sharding import PartitionSpec as P

highest_mode = lax.Precision.HIGHEST


def from_behind(value, axis, steps):
    count = lax.axis_size(axis)
    first, last = (max(0, -steps), min(count, count - steps))
    return lax.ppermute(value, axis, [(source, source + steps) for source in range(first, last)])


def with_halo(array, sides, width):
    for axis, dim in sides:
        devices, length = (lax.axis_size(axis), array.shape[dim])
        up = [(i, (i + 1) % devices) for i in range(devices - 1)]
        down = [(j, i) for i, j in up]
        last = lax.slice_in_dim(array, length - width, length, axis=dim)
        first = lax.slice_in_dim(array, 0, width, axis=dim)
        before = lax.ppermute(last, axis, up)
        after = lax.ppermute(first, axis, down)
        array = jnp.concatenate([before, array, after], axis=dim)
    return array


def einsum_exact(form, first, second):
    return jnp.einsum(form, first, second, precision=highest_mode)


def make_tables(taps, width):
    reach = taps.shape[1] // 2
    pixel_idx = lax.iota(jnp.int32, width)
    offset = pixel_idx[None, :] - pixel_idx[:, None] + reach
    tap_idx = lax.iota(jnp.int32, taps.shape[1])
    one_hot = (offset[:, :, None] == tap_idx[None, None, :]).astype(jnp.float32)
    band_re = einsum_exact("abt,t->ab", one_hot, taps[0])
    band_im = einsum_exact("abt,t->ab", one_hot, taps[1])
    phase_idx = pixel_idx[:, None] * pixel_idx[None, :] % width
    angle = 2.0 * math.pi / width * phase_idx.astype(jnp.float32)
    norm_factor = 1.0 / math.sqrt(width)
    return (band_re, band_im, jnp.cos(angle) * norm_factor, -jnp.sin(angle) * norm_factor)


def both_sides(mat_re, mat_im, wave_re, wave_im):
    left_re = einsum_exact("ab,kbc->kac", mat_re, wave_re) - einsum_exact(
        "ab,kbc->kac", mat_im, wave_im
    )
    left_im = einsum_exact("ab,kbc->kac", mat_re, wave_im) + einsum_exact(
        "ab,kbc->kac", mat_im, wave_re
    )
    out_re = einsum_exact("kac,dc->kad", left_re, mat_re) - einsum_exact(
        "kac,dc->kad", left_im, mat_im
    )
    out_im = einsum_exact("kac,dc->kad", left_re, mat_im) + einsum_exact(
        "kac,dc->kad", left_im, mat_re
    )
    return (out_re, out_im)


def record_loss(probe, patch, measured_one, tables):
    band_re, band_im, dft_re, dft_im = tables
    wave_re = probe[:, 0]
    wave_im = probe[:, 1]
    layers = patch.shape[0]
    for layer_idx in range(layers):
        obj_re = patch[layer_idx, 0]
        obj_im = patch[layer_idx, 1]
        wave_re, wave_im = (
            wave_re * obj_re - wave_im * obj_im,
            wave_re * obj_im + wave_im * obj_re,
        )
        if layer_idx + 1 < layers:
            wave_re, wave_im = both_sides(band_re, band_im, wave_re, wave_im)
    far_re, far_im = both_sides(dft_re, dft_im, wave_re, wave_im)
    intensity = jnp.sum(far_re * far_re + far_im * far_im, axis=0)
    weight = 1.0 / (8.0 * probe.shape[0])
    return 0.5 * weight * jnp.sum((intensity - measured_one) ** 2)


def accumulate(grid, probe, measured, places, tables, patch_width):
    sizes = (grid.shape[0], 2, patch_width, patch_width)

    def one_record(carry, item):
        grad_grid, grad_probe = carry
        place, measured_one = item
        zero_idx = jnp.zeros((), jnp.int32)
        starts = (zero_idx, zero_idx, place[0], place[1])
        patch = lax.dynamic_slice(grid, starts, sizes)
        grad_wave, grad_patch = jax.grad(record_loss, argnums=(0, 1))(
            probe, patch, measured_one, tables
        )
        current = lax.dynamic_slice(grad_grid, starts, sizes)
        grad_grid = lax.dynamic_update_slice(grad_grid, current + grad_patch, starts)
        return ((grad_grid, grad_probe + grad_wave), None)

    init = (jnp.zeros(grid.shape, jnp.float32), jnp.zeros(probe.shape, jnp.float32))
    (grad_grid, grad_probe), unused = lax.scan(one_record, init, (places, measured))
    return (grad_grid, grad_probe)


def gram_of(first, second):
    stacked = jnp.concatenate([first, second], axis=0)
    col_re = stacked[:, 0]
    col_im = stacked[:, 1]
    gram_re = einsum_exact("ax,bx->ab", col_re, col_re) + einsum_exact("ax,bx->ab", col_im, col_im)
    gram_im = einsum_exact("ax,bx->ab", col_re, col_im) - einsum_exact("ax,bx->ab", col_im, col_re)
    return (gram_re, gram_im)


def complex_cholesky(herm_re, herm_im):
    count = herm_re.shape[0]
    order_idx = lax.iota(jnp.int32, count)
    cols_re = []
    cols_im = []
    for col_idx in range(count):
        numer_re = herm_re[:, col_idx]
        numer_im = herm_im[:, col_idx]
        for prev_idx in range(col_idx):
            vec_re = cols_re[prev_idx]
            vec_im = cols_im[prev_idx]
            pivot_re = vec_re[col_idx]
            pivot_im = vec_im[col_idx]
            numer_re = numer_re - (vec_re * pivot_re + vec_im * pivot_im)
            numer_im = numer_im - (vec_im * pivot_re - vec_re * pivot_im)
        diag_val = jnp.sqrt(numer_re[col_idx])
        below = order_idx > col_idx
        at_diag = order_idx == col_idx
        cols_re.append(
            jnp.where(below, numer_re / diag_val, 0.0) + jnp.where(at_diag, diag_val, 0.0)
        )
        cols_im.append(jnp.where(below, numer_im / diag_val, 0.0))
    return (jnp.stack(cols_re, axis=1), jnp.stack(cols_im, axis=1))


def lower_inverse(low_re, low_im):
    count = low_re.shape[0]
    unit = jnp.eye(count, dtype=low_re.dtype)
    rows_re = []
    rows_im = []
    for row_idx in range(count):
        acc_re = unit[row_idx]
        acc_im = jnp.zeros_like(unit[row_idx])
        for prev_idx in range(row_idx):
            coef_re = low_re[row_idx, prev_idx]
            coef_im = low_im[row_idx, prev_idx]
            acc_re = acc_re - (coef_re * rows_re[prev_idx] - coef_im * rows_im[prev_idx])
            acc_im = acc_im - (coef_re * rows_im[prev_idx] + coef_im * rows_re[prev_idx])
        rows_re.append(acc_re / low_re[row_idx, row_idx])
        rows_im.append(acc_im / low_re[row_idx, row_idx])
    return (jnp.stack(rows_re, axis=0), jnp.stack(rows_im, axis=0))


def orthonormalize(probe_cols, grad_cols, gram_re, gram_im, scale_out):
    modes = probe_cols.shape[0]
    trace_pp = jnp.trace(gram_re[:modes, :modes])
    trace_gg = jnp.trace(gram_re[modes:, modes:])
    factor = 0.5 * jnp.sqrt(trace_pp / (trace_gg + 1e-06))
    new_re = (
        gram_re[:modes, :modes]
        - factor * (gram_re[:modes, modes:] + gram_re[modes:, :modes])
        + factor * factor * gram_re[modes:, modes:]
    )
    new_im = (
        gram_im[:modes, :modes]
        - factor * (gram_im[:modes, modes:] + gram_im[modes:, :modes])
        + factor * factor * gram_im[modes:, modes:]
    )
    low_re, low_im = complex_cholesky(new_re, new_im)
    inv_re, inv_im = lower_inverse(low_re, low_im)
    right_re = inv_re.T
    right_im = -inv_im.T
    moved = probe_cols - factor * grad_cols
    moved_re = moved[:, 0]
    moved_im = moved[:, 1]
    out_re = einsum_exact("kx,kj->jx", moved_re, right_re) - einsum_exact(
        "kx,kj->jx", moved_im, right_im
    )
    out_im = einsum_exact("kx,kj->jx", moved_re, right_im) + einsum_exact(
        "kx,kj->jx", moved_im, right_re
    )
    return jnp.stack([out_re, out_im], axis=1) * scale_out


def fold_axis(grad, dim, half):
    full = grad.shape[dim]
    inner = full - 2 * half
    core = lax.slice_in_dim(grad, half, half + inner, axis=dim)
    for step_by in (1, -1):
        if step_by == 1:
            sent = lax.slice_in_dim(grad, half + inner, full, axis=dim)
        else:
            sent = lax.slice_in_dim(grad, 0, half, axis=dim)
        if dim == 2:
            arrived = from_behind(sent, "row", step_by)
        else:
            arrived = from_behind(sent, "col", step_by)
        widths = [(0, 0)] * grad.ndim
        if step_by == 1:
            widths[dim] = (0, inner - half)
        else:
            widths[dim] = (inner - half, 0)
        core = core + jnp.pad(arrived, widths)
    return core


def per_device(object_slices, probe, taps, measured, positions):
    width = probe.shape[-1]
    half = width // 2
    tile_rows = object_slices.shape[2]
    tile_cols = object_slices.shape[3]
    tables = make_tables(taps, width)
    extended = with_halo(object_slices, (("row", 2), ("col", 3)), half)
    anchor = jnp.stack(
        [lax.axis_index("row") * tile_rows - half, lax.axis_index("col") * tile_cols - half]
    )
    places = positions - anchor[None, :]
    grad_ext, grad_probe = accumulate(extended, probe, measured, places, tables, width)
    folded = fold_axis(fold_axis(grad_ext, 2, half), 3, half)
    modes = probe.shape[0]
    pixels = width * width
    probe_cols = probe.reshape(modes, 2, pixels)
    grad_cols = grad_probe.reshape(modes, 2, pixels)
    share = pixels // (lax.axis_size("row") * lax.axis_size("col"))
    start = lax.axis_index(("row", "col")) * share
    own_probe = lax.dynamic_slice_in_dim(probe_cols, start, share, 2)
    total_grad = lax.psum(grad_cols, ("row", "col"))
    gram_re, gram_im = gram_of(probe_cols, total_grad)
    own_grad = lax.dynamic_slice_in_dim(total_grad, start, share, 2)
    new_probe = orthonormalize(own_probe, own_grad, gram_re, gram_im, float(width))
    return (folded, new_probe)


def solution(mesh):
    placed = (
        P(None, None, ("groups", "row"), "col"),
        P("groups", None, None, None),
        P(),
        P(("groups", "row", "col"), None, None),
        P(("groups", "row", "col"), None),
    )
    return jax.shard_map(
        per_device,
        mesh=mesh,
        in_specs=placed,
        out_specs=(P(None, None, ("groups", "row"), "col"), P("groups", None, ("row", "col"))),
        check_vma=False,
    )
```

profile of v0, /device:TPU:0, one launch (start us, length us, event | category | flops | bytes accessed | tf_op | source)
XLA Modules:
  0.0 651.3 jit_solution(16764180511014686650)
XLA Ops:
  8.5 4.9 collective-permute-start
  18.0 17.8 %collective-permute-done = f32[4,2,64,256]{3,2,1,0:T(8,128)S(1)} collective-permute-done((f32[4,2,64,256]{3,2,1,0:T(8,128)S(1)}, f32[4,2,64,256]{3,2,1,0:T(8,128)S(1)}, u32[]{:S(2)}, u32[]{:S(2)}) %collective-permute-start) | collective-permute-done | bytes 524320 | tf_op jit(solution)/shard_map/ppermute | solution.py:23
  56.2 173.7 %while.16 = (s32[]{:T(128)}, f32[4,2,256,384]{3,2,1,0:T(8,128)}, f32[8,2,128,128]{2,3,0,1:T(8,128)}, s32[2,2]{1,0:T(2,128)S(1)}, f32[8,2,128,128]{2,3,0,1:T(8,12...) while((s32[]{:T(128)}, f32[4,2,256,384]{3,2,1,0:T(8,128)}, ...), condition=%wide.region_18.19_spmd.clone.clone, body=%wide.region_0.18_spmd.clone.clone.sunk | while | flops 12914802688 | bytes 137233312 | solution.py:100
  131.2 7.7 %dynamic_update_slice.9 = f32[4,2,256,384]{3,2,1,0:T(8,128)} dynamic-update-slice(f32[4,2,256,384]{3,2,1,0:T(8,128)} %get-tuple-element.615, f32[4,2,128,128]{3,2,1,0:T(8,128)S(1)} %add_add_fusion.2, s32[]{:T(128)} %constant.94.clone.1..sunk, s32[]{:T(128)} %constant.94.clone.1..sunk, s32[]{:T(128)S(6)} %select_n.471, s32[]{:T(128)S(6)} %select_n.472) | dynamic-update-slice | bytes 1048580 | tf_op jit(solution)/shard_map/while/body/eval_jaxpr/dynamic_update_slice | solution.py:96
  215.2 7.2 %dynamic_update_slice.9 = f32[4,2,256,384]{3,2,1,0:T(8,128)} dynamic-update-slice(f32[4,2,256,384]{3,2,1,0:T(8,128)} %get-tuple-element.615, f32[4,2,128,128]{3,2,1,0:T(8,128)S(1)} %add_add_fusion.2, s32[]{:T(128)} %constant.94.clone.1..sunk, s32[]{:T(128)} %constant.94.clone.1..sunk, s32[]{:T(128)S(6)} %select_n.471, s32[]{:T(128)S(6)} %select_n.472) | dynamic-update-slice | bytes 1048580 | tf_op jit(solution)/shard_map/while/body/eval_jaxpr/dynamic_update_slice | solution.py:96
  236.1 5.0 collective-permute-start.4
  242.4 91.3 %all-reduce.16.cloned.1.call-done = f32[8,2,16384]{2,0,1:T(8,128)} async-done(((f32[8,2,16384]{2,0,1:T(8,128)}), f32[8,2,16384]{2,0,1:T(8,128)}) %all-reduce.16.cloned.1.call-update) | async-done | bytes 1048592 | tf_op jit(solution)/shard_map/psum | solution.py:229
  368.6 3.8 compare_select_fusion.15
  375.1 5.0 fusion.282
  381.5 5.1 compare_select_fusion.13
  389.2 6.2 add_subtract_fusion.2
  396.6 6.2 compare_select_fusion.11
  405.3 7.6 %add_subtract_fusion.1 = f32[8]{0:T(128)S(1)} fusion(f32[8]{0:T(128)S(1)} %compare_select_fusion.11, f32[8]{0:T(128)S(1)} %compare_select_fusion.13, f32[8]{0:T(128)S(1)} %compare_select_fusion.15, f32[8]{0:T(128)S(1)} %compare_select_fusion.17, f32[8]{0:T(128)S(1)} %compare_select_fusion.19, f32[8]{0:T(128)S(1)} %get-tuple-element.459, ...), kind=kLoop, calls=%fused_computation.455 | loop fusion | flops 432 | bytes 516 | tf_op jit(solution)/shard_map/sub | solution.py:126
  414.2 7.6 %compare_select_fusion.9 = f32[8]{0:T(128)S(1)} fusion(f32[8]{0:T(128)S(1)} %compare_select_fusion.11, f32[8]{0:T(128)S(1)} %compare_select_fusion.13, f32[8]{0:T(128)S(1)} %compare_select_fusion.15, f32[8]{0:T(128)S(1)} %compare_select_fusion.17, f32[8]{0:T(128)S(1)} %compare_select_fusion.19, f32[8]{0:T(128)S(1)} %get-tuple-element.460, ...), kind=kLoop, calls=%fused_computation.391 | loop fusion | flops 456 | bytes 520 | tf_op jit(solution)/shard_map/jit(_where)/select_n | solution.py:134
  423.6 8.8 %add_subtract_fusion = f32[8]{0:T(128)S(1)} fusion(f32[8]{0:T(128)S(1)} %compare_select_fusion.9, f32[8]{0:T(128)S(1)} %compare_select_fusion.11, f32[8]{0:T(128)S(1)} %compare_select_fusion.13, f32[8]{0:T(128)S(1)} %compare_select_fusion.15, f32[8]{0:T(128)S(1)} %compare_select_fusion.17, f32[8]{0:T(128)S(1)} %compare_select_fusion.19, ...), kind=kLoop, calls=%fused_computation.454 | loop fusion | flops 512 | bytes 592 | tf_op jit(solution)/shard_map/sub | solution.py:126
  434.1 39.2 %subtract_divide_fusion.1 = (f32[1,8]{0,1:T(8,128)S(1)}, f32[1,8]{0,1:T(8,128)S(1)}, f32[1,8]{0,1:T(8,128)S(1)}, f32[1,8]{0,1:T(8,128)S(1)}, f32[1,8]{0,1:T(8,128)S(1)}) fusion(f32[8,8]{0,1:T(8,128)S(1)} %fusion.251, f32[]{:T(128)} %bitcast.99, f32[]{:T(128)} %bitcast.67, f32[]{:T(128)S(6)} %mul.2504, f32[]{:T(128)} %bitcast.96, f32[]{:T(128)} %bitcast.94, ...), kind=kLoop, calls=%fused_computation.360 | loop fusion | flops 1576 | bytes 720 | tf_op jit(solution)/shard_map/div | solution.py:151
  473.4 27.4 %subtract_divide_fusion.3 = f32[1,8]{0,1:T(8,128)S(1)} fusion(f32[]{:T(128)} %bitcast.81, f32[1,8]{0,1:T(8,128)S(1)} %get-tuple-element.353, f32[1,8]{0,1:T(8,128)S(1)} %get-tuple-element.354, f32[1,8]{0,1:T(8,128)S(1)} %get-tuple-element.355, f32[1,8]{0,1:T(8,128)S(1)} %get-tuple-element.356, f32[]{:T(128)} %bitcast.53, f32[8,8]{0,1:T(8,128)S(1)} %fusion.251, ...), kind=kLoop, calls=%fused_computation.362 | loop fusion | flops 960 | bytes 464 | tf_op jit(solution)/shard_map/div | solution.py:151
  500.8 19.0 %subtract_divide_fusion.5 = f32[1,8]{0,1:T(8,128)S(1)} fusion(f32[1,8]{0,1:T(8,128)S(1)} %get-tuple-element.354, f32[1,8]{0,1:T(8,128)S(1)} %get-tuple-element.355, f32[1,8]{0,1:T(8,128)S(1)} %get-tuple-element.356, f32[1,8]{0,1:T(8,128)S(1)} %get-tuple-element.353, f32[8,8]{0,1:T(8,128)S(1)} %fusion.251, f32[]{:T(128)} %bitcast.65, f32[]{:T(128)} %bitcast.41, ...), kind=kLoop, calls=%fused_computation.365 | loop fusion | flops 608 | bytes 372 | tf_op jit(solution)/shard_map/div | solution.py:151
  519.8 12.3 %subtract_divide_fusion.7 = f32[1,8]{0,1:T(8,128)S(1)} fusion(f32[1,8]{0,1:T(8,128)S(1)} %get-tuple-element.353, f32[1,8]{0,1:T(8,128)S(1)} %get-tuple-element.354, f32[1,8]{0,1:T(8,128)S(1)} %get-tuple-element.355, f32[1,8]{0,1:T(8,128)S(1)} %get-tuple-element.356, f32[8,8]{0,1:T(8,128)S(1)} %fusion.251, f32[]{:T(128)} %bitcast.51, f32[]{:T(128)} %bitcast.31, ...), kind=kLoop, calls=%fused_computation.368 | loop fusion | flops 320 | bytes 288 | tf_op jit(solution)/shard_map/div | solution.py:151
  532.7 27.3 %subtract_divide_fusion.2 = f32[1,8]{0,1:T(8,128)S(1)} fusion(f32[1,8]{0,1:T(8,128)S(1)} %get-tuple-element.353, f32[1,8]{0,1:T(8,128)S(1)} %get-tuple-element.354, f32[1,8]{0,1:T(8,128)S(1)} %get-tuple-element.355, f32[1,8]{0,1:T(8,128)S(1)} %get-tuple-element.356, f32[]{:T(128)} %bitcast.67, f32[]{:T(128)S(6)} %mul.2504, f32[]{:T(128)} %bitcast.81, ...), kind=kLoop, calls=%fused_computation.361 | loop fusion | flops 960 | bytes 432 | tf_op jit(solution)/shard_map/div | solution.py:152
  559.9 19.0 %subtract_divide_fusion.4 = f32[1,8]{0,1:T(8,128)S(1)} fusion(f32[1,8]{0,1:T(8,128)S(1)} %get-tuple-element.353, f32[1,8]{0,1:T(8,128)S(1)} %get-tuple-element.354, f32[1,8]{0,1:T(8,128)S(1)} %get-tuple-element.355, f32[1,8]{0,1:T(8,128)S(1)} %get-tuple-element.356, f32[]{:T(128)} %bitcast.53, f32[]{:T(128)S(6)} %mul.2430, f32[]{:T(128)} %bitcast.65, ...), kind=kLoop, calls=%fused_computation.363 | loop fusion | flops 608 | bytes 340 | tf_op jit(solution)/shard_map/div | solution.py:152
  578.9 7.2 %subtract_divide_fusion.8 = (f32[1,8]{0,1:T(8,128)S(1)}, f32[1,8]{0,1:T(8,128)S(1)}, f32[1,8]{0,1:T(8,128)S(1)}) fusion(f32[1,8]{0,1:T(8,128)S(1)} %get-tuple-element.354, f32[1,8]{0,1:T(8,128)S(1)} %get-tuple-element.355, f32[1,8]{0,1:T(8,128)S(1)} %get-tuple-element.356, f32[]{:T(128)} %bitcast.31, f32[]{:T(128)S(6)} %mul.2318, f32[]{:T(128)} %bitcast.39, ...), kind=kLoop, calls=%fused_computation.369 | loop fusion | flops 192 | bytes 252 | tf_op jit(solution)/shard_map/div | solution.py:152
  586.1 36.6 %subtract_divide_fusion = f32[1,8]{0,1:T(8,128)S(1)} fusion(f32[1,8]{0,1:T(8,128)S(1)} %get-tuple-element.353, f32[1,8]{0,1:T(8,128)S(1)} %get-tuple-element.354, f32[1,8]{0,1:T(8,128)S(1)} %get-tuple-element.355, f32[1,8]{0,1:T(8,128)S(1)} %get-tuple-element.356, f32[]{:T(128)} %bitcast.83, f32[]{:T(128)S(6)} %mul.2550, f32[]{:T(128)} %bitcast.99, ...), kind=kLoop, calls=%fused_computation.359 | loop fusion | flops 1376 | bytes 532 | tf_op jit(solution)/shard_map/div | solution.py:152
  622.8 12.2 %subtract_divide_fusion.6 = f32[1,8]{0,1:T(8,128)S(1)} fusion(f32[1,8]{0,1:T(8,128)S(1)} %get-tuple-element.353, f32[1,8]{0,1:T(8,128)S(1)} %get-tuple-element.354, f32[1,8]{0,1:T(8,128)S(1)} %get-tuple-element.355, f32[1,8]{0,1:T(8,128)S(1)} %get-tuple-element.356, f32[]{:T(128)} %bitcast.41, f32[]{:T(128)S(6)} %mul.2368, f32[]{:T(128)} %bitcast.51, ...), kind=kLoop, calls=%fused_computation.366 | loop fusion | flops 320 | bytes 256 | tf_op jit(solution)/shard_map/div | solution.py:152
  (347 shorter events, 218.5 us)
Async XLA Ops:
  7.2 326.5 %all-reduce.16.cloned.1.call-start = ((), (), s32[]{:S(2)}) async-start(), calls=%async_computation | async-start | bytes 2097152 | tf_op jit(solution)/shard_map/psum | solution.py:229
  8.5 27.2 %collective-permute-start = (f32[4,2,64,256]{3,2,1,0:T(8,128)S(1)}, f32[4,2,64,256]{3,2,1,0:T(8,128)S(1)}, u32[]{:S(2)}, u32[]{:S(2)}) collective-permute-start(f32[4,2,64,256]{3,2,1,0:T(8,128)S(1)} %get-tuple-element.392), channel_id=1, source_target_pairs={{0,2},{2,4},{4,6},{6,8},{8,10},{10,12},{12,14},{1,3},{3,5},{5,7},{... | collective-permute-start | bytes 1572872 | tf_op jit(solution)/shard_map/ppermute | solution.py:23
  13.4 22.7 %collective-permute-start.1 = (f32[4,2,64,256]{3,2,1,0:T(8,128)S(1)}, f32[4,2,64,256]{3,2,1,0:T(8,128)}, u32[]{:S(2)}, u32[]{:S(2)}) collective-permute-start(f32[4,2,64,256]{3,2,1,0:T(8,128)S(1)} %get-tuple-element.393), channel_id=1, source_target_pairs={{2,0},{4,2},{6,4},{8,6},{10,8},{12,10},{14,12},{3,1},{5,3},{7,5},{... | collective-permute-start | bytes 1572872 | tf_op jit(solution)/shard_map/ppermute | solution.py:24
  36.1 6.2 copy-start.23
  37.5 4.9 copy-start.9
  37.5 6.4 copy-start.24
  39.0 11.5 %collective-permute-start.2 = (f32[4,2,256,64]{2,3,1,0:T(8,128)}, f32[4,2,256,64]{2,3,1,0:T(8,128)}, u32[]{:S(2)}, u32[]{:S(2)}) collective-permute-start(f32[4,2,256,64]{2,3,1,0:T(8,128)} %get-tuple-element.388), channel_id=1, source_target_pairs={{0,1},{2,3},{4,5},{6,7},{8,9},{10,11},{12,13},{14,15},{16,17},{18,... | collective-permute-start | bytes 1572872 | tf_op jit(solution)/shard_map/ppermute | solution.py:23
  41.1 9.5 %collective-permute-start.3 = (f32[4,2,256,64]{2,3,1,0:T(8,128)}, f32[4,2,256,64]{2,3,1,0:T(8,128)}, u32[]{:S(2)}, u32[]{:S(2)}) collective-permute-start(f32[4,2,256,64]{2,3,1,0:T(8,128)} %get-tuple-element.389), channel_id=1, source_target_pairs={{1,0},{3,2},{5,4},{7,6},{9,8},{11,10},{13,12},{15,14},{17,16},{19,... | collective-permute-start | bytes 1572872 | tf_op jit(solution)/shard_map/ppermute | solution.py:24
  44.0 6.6 %copy-start.10 = (f32[4,2,64,256]{2,3,1,0:T(8,128)S(1)}, f32[4,2,64,256]{2,3,1,0:T(8,128)}, u32[]{:S(2)}) copy-start(f32[4,2,64,256]{2,3,1,0:T(8,128)} %copy-done.9) | copy-start | bytes 1572868
  56.7 9.2 %copy-start = (f32[8,2,128,128]{2,3,0,1:T(8,128)}, f32[8,2,128,128]{2,3,0,1:T(8,128)S(1)}, u32[]{:S(2)}) copy-start(f32[8,2,128,128]{2,3,0,1:T(8,128)S(1)} %get-tuple-element.634) | copy-start | bytes 3145732 | tf_op jit(solution)/shard_map/while
  90.6 4.4 copy-start.2
  90.6 4.4 copy-start.3
  97.4 4.5 copy-start.22
  139.2 9.2 %copy-start = (f32[8,2,128,128]{2,3,0,1:T(8,128)}, f32[8,2,128,128]{2,3,0,1:T(8,128)S(1)}, u32[]{:S(2)}) copy-start(f32[8,2,128,128]{2,3,0,1:T(8,128)S(1)} %get-tuple-element.634) | copy-start | bytes 3145732 | tf_op jit(solution)/shard_map/while
  173.3 4.4 copy-start.2
  173.3 4.4 copy-start.3
  180.0 4.5 copy-start.22
  209.5 3.7 copy-start.11
  209.5 3.7 copy-start.12
  236.1 399.5 %collective-permute-start.4 = (f32[4,2,64,384]{3,2,1,0:T(8,128)}, f32[4,2,64,384]{3,2,1,0:T(8,128)S(1)}, u32[]{:S(2)}, u32[]{:S(2)}) collective-permute-start(f32[4,2,64,384]{3,2,1,0:T(8,128)} %get-tuple-element.386), channel_id=1, source_target_pairs={{0,2},{2,4},{4,6},{6,8},{8,10},{10,12},{12,14},{1,3},{3,5},{5,7},{... | collective-permute-start | bytes 2359304 | tf_op jit(solution)/shard_map/ppermute | solution.py:13
  241.1 394.5 %collective-permute-start.5 = (f32[4,2,64,384]{3,2,1,0:T(8,128)}, f32[4,2,64,384]{3,2,1,0:T(8,128)}, u32[]{:S(2)}, u32[]{:S(2)}) collective-permute-start(f32[4,2,64,384]{3,2,1,0:T(8,128)} %get-tuple-element.387), channel_id=1, source_target_pairs={{2,0},{4,2},{6,4},{8,6},{10,8},{12,10},{14,12},{3,1},{5,3},{7,5},{... | collective-permute-start | bytes 2359304 | tf_op jit(solution)/shard_map/ppermute | solution.py:13
  333.7 8.8 %copy-start.8 = (f32[8,2,16384]{2,0,1:T(8,128)S(1)}, f32[8,2,16384]{2,0,1:T(8,128)}, u32[]{:S(2)}) copy-start(f32[8,2,16384]{2,0,1:T(8,128)} %all-reduce.16.cloned.1.call-done) | copy-start | bytes 3145732
  637.7 3.8 collective-permute-start.6
  639.0 3.8 collective-permute-start.7
  (29 other events, 75.8 us)
Sparse Core Ops, SparseCore 0:
  232.9 100.7 all-reduce.15
where the time goes:
time: 663 us; the launch traced here: 651 us
  other arithmetic  279 us (42%)
  matrix products  135 us (20%)
  waiting for transfers between devices  110 us (17%)
  local copies, waits for them, and re-layouts  59.8 us (9%)
  between operations  30.9 us (5%)
  starting transfers between devices  18.4 us (3%)
  loops' own time  17.8 us (3%)
    dot_general x138, matrix products, einsum_exact(): return jnp.einsum(form, first, second, precision=highest_mode)  135 us
    div x5, other arithmetic, lower_inverse(): rows_im.append(acc_im / low_re[row_idx, row_idx])  102 us
    div x4, other arithmetic, lower_inverse(): rows_re.append(acc_re / low_re[row_idx, row_idx])  97.9 us
    psum x1, waiting for transfers between devices, per_device(): total_grad = lax.psum(grad_cols, ('row', 'col'))  91.3 us
    sub x7, other arithmetic, complex_cholesky(): numer_re = numer_re - (vec_re * pivot_re + vec_im * pivot_im)  34.9 us
    select_n x7, other arithmetic, complex_cholesky(): cols_im.append(jnp.where(below, numer_im / diag_val, 0.0))  26.1 us
    another operation x1, loops' own time, accumulate(): lax.scan(one_record, init, (places, measured))  17.8 us
    ppermute x2, waiting for transfers between devices, with_halo(): before = lax.ppermute(last, axis, up)  17.8 us
  transfers between devices with their start and end apart: 9, of which 3 were waited for; matrix products, arithmetic and copies ran while one was open for 46% of the time, Pallas kernels for 0%

commit v1 on v0

--- a/solution.py
+++ b/solution.py
@@ -226,7 +226,8 @@
     share = pixels // (lax.axis_size("row") * lax.axis_size("col"))
     start = lax.axis_index(("row", "col")) * share
     own_probe = lax.dynamic_slice_in_dim(probe_cols, start, share, 2)
-    total_grad = lax.psum(grad_cols, ("row", "col"))
+    blocks = lax.all_gather(grad_cols, ("row", "col"))
+    total_grad = jnp.sum(blocks, axis=0)
     gram_re, gram_im = gram_of(probe_cols, total_grad)
     own_grad = lax.dynamic_slice_in_dim(total_grad, start, share, 2)
     new_probe = orthonormalize(own_probe, own_grad, gram_re, gram_im, float(width))

time: 663 us -> 706 us (1.065)
  waiting for transfers between devices: 110 us -> 146 us
  other arithmetic: 279 us -> 287 us
    psum x1 -> x0, waiting for transfers between devices: 91.3 us -> none  [per_device(): total_grad = lax.psum(grad_cols, ('row', 'col'))]
    all_gather x0 -> x1, waiting for transfers between devices: none -> 86.4 us  [per_device(): blocks = lax.all_gather(grad_cols, ('row', 'col'))]
    ppermute x4, waiting for transfers between devices: 1.35 us -> 43.1 us  [from_behind(): lax.ppermute(value, axis, [(source, source + steps) for source in range(f...]
  transfers between devices with their start and end apart: 9 -> 9, of which waited for: 3 -> 6; matrix products, arithmetic and copies ran while one was open for 46% -> 2% of each run, Pallas kernels for 0% -> 0%
where the time goes in v1:
time: 706 us; the launch traced here: 695 us
  other arithmetic  287 us (41%)
  waiting for transfers between devices  146 us (21%)
  matrix products  130 us (18%)
  local copies, waits for them, and re-layouts  58.2 us (8%)
  between operations  30.8 us (4%)
  starting transfers between devices  25 us (4%)
  loops' own time  18.3 us (3%)
    dot_general x138, matrix products, einsum_exact(): return jnp.einsum(form, first, second, precision=highest_mode)  130 us
    div x5, other arithmetic, lower_inverse(): rows_im.append(acc_im / low_re[row_idx, row_idx])  103 us
    div x4, other arithmetic, lower_inverse(): rows_re.append(acc_re / low_re[row_idx, row_idx])  98.3 us
    all_gather x1, waiting for transfers between devices, per_device(): blocks = lax.all_gather(grad_cols, ('row', 'col'))  86.4 us
    ppermute x4, waiting for transfers between devices, from_behind(): lax.ppermute(value, axis, [(source, source + steps) for source in range(f...  43.1 us
    sub x7, other arithmetic, complex_cholesky(): numer_re = numer_re - (vec_re * pivot_re + vec_im * pivot_im)  35.1 us
    select_n x7, other arithmetic, complex_cholesky(): cols_im.append(jnp.where(below, numer_im / diag_val, 0.0))  26.1 us
    another operation x1, loops' own time, accumulate(): lax.scan(one_record, init, (places, measured))  18.3 us
  transfers between devices with their start and end apart: 9, of which 6 were waited for; matrix products, arithmetic and copies ran while one was open for 2% of the time, Pallas kernels for 0%

profile of v1, /device:TPU:0, one launch (start us, length us, event | category | flops | bytes accessed | tf_op | source)
XLA Modules:
  0.0 695.2 jit_solution(5207896359924296557)
XLA Ops:
  9.8 6.3 collective-permute-start
  19.4 5.9 collective-permute-done.1
  25.6 11.0 %collective-permute-done = f32[4,2,64,256]{3,2,1,0:T(8,128)} collective-permute-done((f32[4,2,64,256]{3,2,1,0:T(8,128)S(1)}, f32[4,2,64,256]{3,2,1,0:T(8,128)}, u32[]{:S(2)}, u32[]{:S(2)}) %collective-permute-start) | collective-permute-done | bytes 524320 | tf_op jit(solution)/shard_map/ppermute | solution.py:23
  59.2 169.8 %while.16 = (s32[]{:T(128)}, f32[4,2,256,384]{3,2,1,0:T(8,128)}, f32[8,2,128,128]{2,3,0,1:T(8,128)}, s32[2,2]{1,0:T(2,128)S(1)}, f32[8,2,128,128]{2,3,0,1:T(8,12...) while((s32[]{:T(128)}, f32[4,2,256,384]{3,2,1,0:T(8,128)}, ...), condition=%wide.region_18.19_spmd.clone.clone, body=%wide.region_0.18_spmd.clone.clone.sunk | while | flops 12914802688 | bytes 135660272 | solution.py:100
  130.9 7.8 %dynamic_update_slice.9 = f32[4,2,256,384]{3,2,1,0:T(8,128)} dynamic-update-slice(f32[4,2,256,384]{3,2,1,0:T(8,128)} %get-tuple-element.615, f32[4,2,128,128]{3,2,1,0:T(8,128)S(1)} %add_add_fusion.2, s32[]{:T(128)} %constant.94.clone.1..sunk, s32[]{:T(128)} %constant.94.clone.1..sunk, s32[]{:T(128)S(6)} %select_n.471, s32[]{:T(128)S(6)} %select_n.472) | dynamic-update-slice | bytes 1048580 | tf_op jit(solution)/shard_map/while/body/eval_jaxpr/dynamic_update_slice | solution.py:96
  211.4 7.2 %dynamic_update_slice.9 = f32[4,2,256,384]{3,2,1,0:T(8,128)} dynamic-update-slice(f32[4,2,256,384]{3,2,1,0:T(8,128)} %get-tuple-element.615, f32[4,2,128,128]{3,2,1,0:T(8,128)S(1)} %add_add_fusion.2, s32[]{:T(128)} %constant.94.clone.1..sunk, s32[]{:T(128)} %constant.94.clone.1..sunk, s32[]{:T(128)S(6)} %select_n.471, s32[]{:T(128)S(6)} %select_n.472) | dynamic-update-slice | bytes 1048580 | tf_op jit(solution)/shard_map/while/body/eval_jaxpr/dynamic_update_slice | solution.py:96
  241.4 24.5 %collective-permute-done.5 = f32[4,2,64,384]{3,2,1,0:T(8,128)S(1)} collective-permute-done((f32[4,2,64,384]{3,2,1,0:T(8,128)S(1)}, f32[4,2,64,384]{3,2,1,0:T(8,128)S(1)}, u32[]{:S(2)}, u32[]{:S(2)}) %collective-permute-start.5) | collective-permute-done | bytes 786464 | tf_op jit(solution)/shard_map/ppermute | solution.py:13
  265.9 17.7 %collective-permute-done.4 = f32[4,2,64,384]{3,2,1,0:T(8,128)S(1)} collective-permute-done((f32[4,2,64,384]{3,2,1,0:T(8,128)S(1)}, f32[4,2,64,384]{3,2,1,0:T(8,128)S(1)}, u32[]{:S(2)}, u32[]{:S(2)}) %collective-permute-start.4) | collective-permute-done | bytes 786464 | tf_op jit(solution)/shard_map/ppermute | solution.py:13
  292.9 86.4 %all-gather.2.cloned.1.call-done = f32[16,8,2,16384]{3,1,2,0:T(8,128)} async-done(((f32[1,8,2,16384]{3,1,2,0:T(8,128)}), f32[16,8,2,16384]{3,1,2,0:T(8,128)}) %all-gather.2.cloned.1.call-update) | async-done | bytes 16777232 | tf_op jit(solution)/shard_map/all_gather | solution.py:229
  379.3 6.6 reduce_sum.293
  432.3 6.0 add_subtract_fusion.2
  439.6 6.0 compare_select_fusion.11
  447.0 7.5 %add_subtract_fusion.1 = f32[8]{0:T(128)S(1)} fusion(f32[8]{0:T(128)S(1)} %compare_select_fusion.11, f32[8]{0:T(128)S(1)} %compare_select_fusion.13, f32[8]{0:T(128)S(1)} %compare_select_fusion.15, f32[8]{0:T(128)S(1)} %compare_select_fusion.17, f32[8]{0:T(128)S(1)} %compare_select_fusion.19, f32[8]{0:T(128)S(1)} %get-tuple-element.459, ...), kind=kLoop, calls=%fused_computation.455 | loop fusion | flops 432 | bytes 516 | tf_op jit(solution)/shard_map/sub | solution.py:126
  455.8 7.5 %compare_select_fusion.9 = f32[8]{0:T(128)S(1)} fusion(f32[8]{0:T(128)S(1)} %compare_select_fusion.11, f32[8]{0:T(128)S(1)} %compare_select_fusion.13, f32[8]{0:T(128)S(1)} %compare_select_fusion.15, f32[8]{0:T(128)S(1)} %compare_select_fusion.17, f32[8]{0:T(128)S(1)} %compare_select_fusion.19, f32[8]{0:T(128)S(1)} %get-tuple-element.460, ...), kind=kLoop, calls=%fused_computation.391 | loop fusion | flops 456 | bytes 520 | tf_op jit(solution)/shard_map/jit(_where)/select_n | solution.py:134
  473.2 9.0 %add_subtract_fusion = f32[8]{0:T(128)S(1)} fusion(f32[8]{0:T(128)S(1)} %compare_select_fusion.9, f32[8]{0:T(128)S(1)} %compare_select_fusion.11, f32[8]{0:T(128)S(1)} %compare_select_fusion.13, f32[8]{0:T(128)S(1)} %compare_select_fusion.15, f32[8]{0:T(128)S(1)} %compare_select_fusion.17, f32[8]{0:T(128)S(1)} %compare_select_fusion.19, ...), kind=kLoop, calls=%fused_computation.454 | loop fusion | flops 512 | bytes 592 | tf_op jit(solution)/shard_map/sub | solution.py:126
  484.2 39.3 %subtract_divide_fusion.1 = (f32[1,8]{0,1:T(8,128)S(1)}, f32[1,8]{0,1:T(8,128)S(1)}, f32[1,8]{0,1:T(8,128)S(1)}, f32[1,8]{0,1:T(8,128)S(1)}, f32[1,8]{0,1:T(8,128)S(1)}) fusion(f32[8,8]{0,1:T(8,128)S(1)} %fusion.251, f32[]{:T(128)} %bitcast.99, f32[]{:T(128)} %bitcast.67, f32[]{:T(128)S(6)} %mul.2504, f32[]{:T(128)} %bitcast.96, f32[]{:T(128)} %bitcast.94, ...), kind=kLoop, calls=%fused_computation.360 | loop fusion | flops 1576 | bytes 720 | tf_op jit(solution)/shard_map/div | solution.py:151
  523.6 7.3 %subtract_divide_fusion.8 = (f32[1,8]{0,1:T(8,128)S(1)}, f32[1,8]{0,1:T(8,128)S(1)}, f32[1,8]{0,1:T(8,128)S(1)}) fusion(f32[1,8]{0,1:T(8,128)S(1)} %get-tuple-element.354, f32[1,8]{0,1:T(8,128)S(1)} %get-tuple-element.355, f32[1,8]{0,1:T(8,128)S(1)} %get-tuple-element.356, f32[]{:T(128)} %bitcast.31, f32[]{:T(128)S(6)} %mul.2318, f32[]{:T(128)} %bitcast.39, ...), kind=kLoop, calls=%fused_computation.369 | loop fusion | flops 192 | bytes 252 | tf_op jit(solution)/shard_map/div | solution.py:152
  530.9 12.5 %subtract_divide_fusion.6 = f32[1,8]{0,1:T(8,128)S(1)} fusion(f32[1,8]{0,1:T(8,128)S(1)} %get-tuple-element.353, f32[1,8]{0,1:T(8,128)S(1)} %get-tuple-element.354, f32[1,8]{0,1:T(8,128)S(1)} %get-tuple-element.355, f32[1,8]{0,1:T(8,128)S(1)} %get-tuple-element.356, f32[]{:T(128)} %bitcast.41, f32[]{:T(128)S(6)} %mul.2368, f32[]{:T(128)} %bitcast.51, ...), kind=kLoop, calls=%fused_computation.366 | loop fusion | flops 320 | bytes 256 | tf_op jit(solution)/shard_map/div | solution.py:152
  543.4 19.2 %subtract_divide_fusion.4 = f32[1,8]{0,1:T(8,128)S(1)} fusion(f32[1,8]{0,1:T(8,128)S(1)} %get-tuple-element.353, f32[1,8]{0,1:T(8,128)S(1)} %get-tuple-element.354, f32[1,8]{0,1:T(8,128)S(1)} %get-tuple-element.355, f32[1,8]{0,1:T(8,128)S(1)} %get-tuple-element.356, f32[]{:T(128)} %bitcast.53, f32[]{:T(128)S(6)} %mul.2430, f32[]{:T(128)} %bitcast.65, ...), kind=kLoop, calls=%fused_computation.363 | loop fusion | flops 608 | bytes 340 | tf_op jit(solution)/shard_map/div | solution.py:152
  562.6 27.2 %subtract_divide_fusion.2 = f32[1,8]{0,1:T(8,128)S(1)} fusion(f32[1,8]{0,1:T(8,128)S(1)} %get-tuple-element.353, f32[1,8]{0,1:T(8,128)S(1)} %get-tuple-element.354, f32[1,8]{0,1:T(8,128)S(1)} %get-tuple-element.355, f32[1,8]{0,1:T(8,128)S(1)} %get-tuple-element.356, f32[]{:T(128)} %bitcast.67, f32[]{:T(128)S(6)} %mul.2504, f32[]{:T(128)} %bitcast.81, ...), kind=kLoop, calls=%fused_computation.361 | loop fusion | flops 960 | bytes 432 | tf_op jit(solution)/shard_map/div | solution.py:152
  590.5 12.6 %subtract_divide_fusion.7 = f32[1,8]{0,1:T(8,128)S(1)} fusion(f32[1,8]{0,1:T(8,128)S(1)} %get-tuple-element.353, f32[1,8]{0,1:T(8,128)S(1)} %get-tuple-element.354, f32[1,8]{0,1:T(8,128)S(1)} %get-tuple-element.355, f32[1,8]{0,1:T(8,128)S(1)} %get-tuple-element.356, f32[8,8]{0,1:T(8,128)S(1)} %fusion.251, f32[]{:T(128)} %bitcast.51, f32[]{:T(128)} %bitcast.31, ...), kind=kLoop, calls=%fused_computation.368 | loop fusion | flops 320 | bytes 288 | tf_op jit(solution)/shard_map/div | solution.py:151
  603.0 19.2 %subtract_divide_fusion.5 = f32[1,8]{0,1:T(8,128)S(1)} fusion(f32[1,8]{0,1:T(8,128)S(1)} %get-tuple-element.354, f32[1,8]{0,1:T(8,128)S(1)} %get-tuple-element.355, f32[1,8]{0,1:T(8,128)S(1)} %get-tuple-element.356, f32[1,8]{0,1:T(8,128)S(1)} %get-tuple-element.353, f32[8,8]{0,1:T(8,128)S(1)} %fusion.251, f32[]{:T(128)} %bitcast.65, f32[]{:T(128)} %bitcast.41, ...), kind=kLoop, calls=%fused_computation.365 | loop fusion | flops 608 | bytes 372 | tf_op jit(solution)/shard_map/div | solution.py:151
  622.3 27.2 %subtract_divide_fusion.3 = f32[1,8]{0,1:T(8,128)S(1)} fusion(f32[]{:T(128)} %bitcast.81, f32[1,8]{0,1:T(8,128)S(1)} %get-tuple-element.353, f32[1,8]{0,1:T(8,128)S(1)} %get-tuple-element.354, f32[1,8]{0,1:T(8,128)S(1)} %get-tuple-element.355, f32[1,8]{0,1:T(8,128)S(1)} %get-tuple-element.356, f32[]{:T(128)} %bitcast.53, f32[8,8]{0,1:T(8,128)S(1)} %fusion.251, ...), kind=kLoop, calls=%fused_computation.362 | loop fusion | flops 960 | bytes 464 | tf_op jit(solution)/shard_map/div | solution.py:151
  649.5 36.8 %subtract_divide_fusion = f32[1,8]{0,1:T(8,128)S(1)} fusion(f32[1,8]{0,1:T(8,128)S(1)} %get-tuple-element.353, f32[1,8]{0,1:T(8,128)S(1)} %get-tuple-element.354, f32[1,8]{0,1:T(8,128)S(1)} %get-tuple-element.355, f32[1,8]{0,1:T(8,128)S(1)} %get-tuple-element.356, f32[]{:T(128)} %bitcast.83, f32[]{:T(128)S(6)} %mul.2550, f32[]{:T(128)} %bitcast.99, ...), kind=kLoop, calls=%fused_computation.359 | loop fusion | flops 1376 | bytes 532 | tf_op jit(solution)/shard_map/div | solution.py:152
  (326 shorter events, 235.1 us)
Async XLA Ops:
  7.2 372.1 %all-gather.2.cloned.1.call-start = ((), (), s32[]{:S(2)}) async-start(), calls=%async_computation | async-start | bytes 17825792 | tf_op jit(solution)/shard_map/all_gather | solution.py:229
  8.5 16.8 %collective-permute-start.1 = (f32[4,2,64,256]{3,2,1,0:T(8,128)S(1)}, f32[4,2,64,256]{3,2,1,0:T(8,128)S(1)}, u32[]{:S(2)}, u32[]{:S(2)}) collective-permute-start(f32[4,2,64,256]{3,2,1,0:T(8,128)S(1)} %get-tuple-element.393), channel_id=1, source_target_pairs={{2,0},{4,2},{6,4},{8,6},{10,8},{12,10},{14,12},{3,1},{5,3},{7,5},{... | collective-permute-start | bytes 1572872 | tf_op jit(solution)/shard_map/ppermute | solution.py:24
  9.8 26.8 %collective-permute-start = (f32[4,2,64,256]{3,2,1,0:T(8,128)S(1)}, f32[4,2,64,256]{3,2,1,0:T(8,128)}, u32[]{:S(2)}, u32[]{:S(2)}) collective-permute-start(f32[4,2,64,256]{3,2,1,0:T(8,128)S(1)} %get-tuple-element.392), channel_id=1, source_target_pairs={{0,2},{2,4},{4,6},{6,8},{8,10},{10,12},{12,14},{1,3},{3,5},{5,7},{... | collective-permute-start | bytes 1572872 | tf_op jit(solution)/shard_map/ppermute | solution.py:23
  25.6 19.8 %copy-start.18 = (s32[2,2]{1,0:T(2,128)S(1)}, s32[2,2]{1,0:T(2,128)}, u32[]{:S(2)}) copy-start(s32[2,2]{1,0:T(2,128)} %param.11) | copy-start | bytes 52
  38.0 7.4 %copy-start.9 = (f32[4,2,64,256]{2,3,1,0:T(8,128)}, f32[4,2,64,256]{2,3,1,0:T(8,128)S(1)}, u32[]{:S(2)}) copy-start(f32[4,2,64,256]{2,3,1,0:T(8,128)S(1)} %copy.329) | copy-start | bytes 1572868
  38.1 8.9 %copy-start.19 = (f32[2,63]{1,0:T(2,128)S(1)}, f32[2,63]{1,0:T(2,128)}, u32[]{:S(2)}) copy-start(f32[2,63]{1,0:T(2,128)} %param.9) | copy-start | bytes 1516
  39.5 14.0 %collective-permute-start.3 = (f32[4,2,256,64]{2,3,1,0:T(8,128)}, f32[4,2,256,64]{2,3,1,0:T(8,128)}, u32[]{:S(2)}, u32[]{:S(2)}) collective-permute-start(f32[4,2,256,64]{2,3,1,0:T(8,128)} %get-tuple-element.389), channel_id=1, source_target_pairs={{1,0},{3,2},{5,4},{7,6},{9,8},{11,10},{13,12},{15,14},{17,16},{19,... | collective-permute-start | bytes 1572872 | tf_op jit(solution)/shard_map/ppermute | solution.py:24
  40.8 12.7 %collective-permute-start.2 = (f32[4,2,256,64]{2,3,1,0:T(8,128)}, f32[4,2,256,64]{2,3,1,0:T(8,128)}, u32[]{:S(2)}, u32[]{:S(2)}) collective-permute-start(f32[4,2,256,64]{2,3,1,0:T(8,128)} %get-tuple-element.388), channel_id=1, source_target_pairs={{0,1},{2,3},{4,5},{6,7},{8,9},{10,11},{12,13},{14,15},{16,17},{18,... | collective-permute-start | bytes 1572872 | tf_op jit(solution)/shard_map/ppermute | solution.py:23
  47.0 6.6 copy-start.10
  59.7 9.6 %copy-start = (f32[8,2,128,128]{2,3,0,1:T(8,128)}, f32[8,2,128,128]{2,3,0,1:T(8,128)S(1)}, u32[]{:S(2)}) copy-start(f32[8,2,128,128]{2,3,0,1:T(8,128)S(1)} %get-tuple-element.634) | copy-start | bytes 3145732 | tf_op jit(solution)/shard_map/while
  92.8 5.5 copy-start.2
  92.8 5.5 copy-start.3
  99.5 4.6 copy-start.17
  139.9 9.6 %copy-start = (f32[8,2,128,128]{2,3,0,1:T(8,128)}, f32[8,2,128,128]{2,3,0,1:T(8,128)S(1)}, u32[]{:S(2)}) copy-start(f32[8,2,128,128]{2,3,0,1:T(8,128)S(1)} %get-tuple-element.634) | copy-start | bytes 3145732 | tf_op jit(solution)/shard_map/while
  146.8 3.4 copy-start.6
  173.2 5.5 copy-start.2
  173.2 5.5 copy-start.3
  179.9 4.6 copy-start.17
  229.0 5.1 copy-start.8
  234.3 31.6 %collective-permute-start.5 = (f32[4,2,64,384]{3,2,1,0:T(8,128)S(1)}, f32[4,2,64,384]{3,2,1,0:T(8,128)S(1)}, u32[]{:S(2)}, u32[]{:S(2)}) collective-permute-start(f32[4,2,64,384]{3,2,1,0:T(8,128)S(1)} %get-tuple-element.387), channel_id=1, source_target_pairs={{2,0},{4,2},{6,4},{8,6},{10,8},{12,10},{14,12},{3,1},{5,3},{7,5},{... | collective-permute-start | bytes 2359304 | tf_op jit(solution)/shard_map/ppermute | solution.py:13
  235.6 52.9 %copy-start.16 = (f32[8,2,128,128]{3,2,1,0:T(8,128)S(1)}, f32[8,2,128,128]{3,2,1,0:T(8,128)}, u32[]{:S(2)}) copy-start(f32[8,2,128,128]{3,2,1,0:T(8,128)} %param.8) | copy-start | bytes 3145732
  235.6 48.1 %collective-permute-start.4 = (f32[4,2,64,384]{3,2,1,0:T(8,128)S(1)}, f32[4,2,64,384]{3,2,1,0:T(8,128)S(1)}, u32[]{:S(2)}, u32[]{:S(2)}) collective-permute-start(f32[4,2,64,384]{3,2,1,0:T(8,128)S(1)} %get-tuple-element.386), channel_id=1, source_target_pairs={{0,2},{2,4},{4,6},{6,8},{8,10},{10,12},{12,14},{1,3},{3,5},{5,7},{... | collective-permute-start | bytes 2359304 | tf_op jit(solution)/shard_map/ppermute | solution.py:13
  284.1 5.1 collective-permute-start.7
  285.4 4.6 collective-permute-start.6
  (18 other events, 52.3 us)
Sparse Core Ops, SparseCore 0:
  234.3 144.9 all-gather.1
